TPU v7x, 128 devices: a whole 4x4x4 slice. The times are simulated.
128 devices in a mesh: rows: 4 (over x), cols: 32 (over y, z, core).
Axes of the slice: x: 4, y: 4, z: 4, core: 2. Of those that a mesh axis runs over, the one named last changes fastest.
Arguments:
- weight: bfloat16 [8192, 16384], P('rows', 'cols'), may hold values from -0.046875 to 0.046875
- hess_inv: float32 [16384, 16384], P('rows', 'cols'), as said below
- selected: int32 [3, 64], replicated, may hold values from 0 to 16383, as said below
- block_mask: int32 [8192, 128], P('rows'), may hold values 0 or 1
- row_limits: int32 [8192], P('rows'), may hold values from 16 to 128
- calibration: bfloat16 [1024, 16384], P(None, 'cols'), may hold values from -6 to 6
Outputs:
- pruned: bfloat16 [8192, 16384], P('rows', 'cols')
- layer_error: float32 [8192, 1024], P('rows', 'cols')
Inputs may be any that keep to these rules, and one draw needn't show every extreme that they name: `selected`: all 192 entries differ; 0 and 16383 are among them. `hess_inv`: symmetric positive definite.
All inputs are finite; a program needn't handle non-finite values. No bound on the sum of `block_mask` on one device may be relied on, other than what follows from the above.
Results may differ from a plain program's by a relative error of at most 0.005.
Values may be sent and summed in bfloat16 or wider, within the bound.
A program may use at most 128 MiB of HBM per device.

v0:
```python
import jax
import jax.numpy as jnp
from jax import lax
from jax.sharding import PartitionSpec as P

BLK = 128


def local(weight, hess_inv, selected, block_mask, row_limits, calibration):
    rows_local, cols_local = hess_inv.shape
    out_local = weight.shape[0]
    group = lax.axis_size("cols")
    row_offset = lax.axis_index("rows") * rows_local
    col_offset = lax.axis_index("cols") * cols_local
    chosen = selected.reshape(-1)
    row_place = chosen - row_offset
    row_inside = (row_place >= 0) & (row_place < rows_local)
    own_rows = jnp.where(
        row_inside[:, None], jnp.take(hess_inv, jnp.clip(row_place, 0, rows_local - 1), axis=0), 0.0
    )
    onehot = (
        lax.broadcasted_iota(jnp.int32, (cols_local, chosen.shape[0]), 0)
        == (chosen - col_offset)[None, :]
    )
    square = lax.psum(
        jnp.dot(own_rows, onehot.astype(jnp.float32), precision=lax.Precision.HIGHEST),
        ("rows", "cols"),
    )
    panel = lax.psum(own_rows, "rows")
    weight_cols = lax.psum(
        jnp.dot(weight, onehot.astype(jnp.bfloat16), preferred_element_type=jnp.float32).astype(
            jnp.bfloat16
        ),
        "cols",
    )
    factor = jnp.linalg.cholesky(square)
    coeffs = jax.scipy.linalg.cho_solve((factor, True), panel)
    wide = weight.astype(jnp.float32)
    refit = wide - jnp.dot(weight_cols.astype(jnp.float32), coeffs, precision=lax.Precision.HIGHEST)
    blocks_local = cols_local // BLK
    running_count = jnp.cumsum(block_mask, axis=1)
    retained = block_mask * (running_count <= row_limits[:, None]).astype(jnp.int32)
    own_blocks = lax.dynamic_slice_in_dim(
        retained, lax.axis_index("cols") * blocks_local, blocks_local, 1
    )
    masked = (
        refit.reshape(out_local, blocks_local, BLK) * own_blocks.astype(jnp.float32)[:, :, None]
    ).reshape(out_local, cols_local)
    pruned = masked.astype(jnp.bfloat16)
    difference = (wide - masked).astype(jnp.bfloat16)
    tokens = calibration.shape[0]
    partial = lax.dot_general(
        calibration.reshape(group, tokens // group, cols_local),
        difference,
        (((2,), (1,)), ((), ())),
        preferred_element_type=jnp.float32,
    ).astype(jnp.bfloat16)
    pieces = lax.all_to_all(partial, "cols", split_axis=0, concat_axis=0, tiled=True)
    layer_error = jnp.sum(pieces.astype(jnp.float32), axis=0).T
    return (pruned, layer_error)


def solution(mesh):
    placed = (
        P("rows", "cols"),
        P("rows", "cols"),
        P(),
        P("rows", None),
        P("rows"),
        P(None, "cols"),
    )
    return jax.shard_map(
        local,
        mesh=mesh,
        in_specs=placed,
        out_specs=(P("rows", "cols"), P("rows", "cols")),
        check_vma=False,
    )
```

profile of v0, /device:TPU:1, one launch (start us, length us, event | category | flops | bytes accessed | tf_op | source)
XLA Modules:
  0.0 391.7 jit_solution(5587726836660570919)
XLA Ops:
  7.2 0.0 all-reduce.9.cloned.1.call-start
  7.2 0.8 compare_and_fusion.1
  8.1 0.7 subtract_clamp_fusion
  8.8 0.1 min.18
  8.9 0.1 min.16
  9.0 0.1 and.20
  9.1 0.1 sub.41
  9.2 5.2 %gather_fusion = f32[192,512]{1,0:T(8,128)} fusion(f32[4096,512]{1,0:T(8,128)} %param.7, s32[1024]{0:T(1024)S(1)} %pad_clamp_fusion), kind=kCustom, calls=%fused_computation | custom fusion | bytes 787200 | tf_op jit(solution)/shard_map/jit(_take)/gather | solution.py:19
  14.3 1.1 select_select_fusion
  15.5 1.3 fusion.5
  16.7 0.0 all-reduce.9.cloned.1.call-update
  16.8 0.0 all-reduce.11.cloned.1.call-start
  16.8 0.7 all-reduce.11.cloned.1.call-update
  17.5 0.0 all-reduce.7.cloned.1.call-start
  17.6 1.8 fusion.2
  19.3 0.0 all-reduce.7.cloned.1.call-update
  19.4 0.6 pad_convert_fusion
  20.0 2.5 copy.10
  22.5 3.1 reduce_window_sum.11
  25.6 0.9 fusion.20
  26.5 1.3 copy.12
  27.8 136.7 %all-reduce.9.cloned.1.call-done = f32[192,192]{0,1:T(8,128)} async-done(((f32[192,192]{0,1:T(8,128)}), f32[192,192]{0,1:T(8,128)}) %all-reduce.9.cloned.1.call-update) | async-done | bytes 147472 | tf_op jit(solution)/shard_map/psum | solution.py:25
  164.5 1.0 copy.9
  165.6 1.0 fusion.15
  166.6 11.7 %cholesky.51 = f32[128,128]{1,0:T(8,128)S(1)} custom-call(f32[128,128]{1,0:T(8,128)S(1)} %cholesky.124), custom_call_target="Cholesky" | custom-call | tf_op jit(solution)/shard_map/jit(cholesky)/cholesky | solution.py:36
  178.3 0.6 compare_reduce_fusion.1
  178.9 10.4 %custom-call.18 = f32[1,128,128]{1,2,0:T(8,128)} custom-call(f32[1,128,128]{2,1,0:T(8,128)S(1)} %get-tuple-element.23), custom_call_target="InvertDiagBlocksLowerTriangular" | custom-call | tf_op jit(solution)/shard_map/jit(cholesky)/cholesky | solution.py:36
  189.4 0.9 cholesky.119
  190.2 1.0 constant_dynamic-update-slice_fusion
  191.3 0.8 convolution_subtract_fusion.2
  192.1 6.6 %cholesky.110 = f32[64,64]{1,0:T(8,128)S(1)} custom-call(f32[64,64]{1,0:T(8,128)} %convolution_subtract_fusion.2), custom_call_target="Cholesky" | custom-call | tf_op jit(solution)/shard_map/jit(cholesky)/cholesky | solution.py:36
  198.7 0.6 compare_reduce_fusion
  200.6 0.9 fusion.16
  201.5 0.7 pad_maximum_fusion
  202.2 20.5 %custom-call.19 = f32[2,128,128]{1,2,0:T(8,128)S(1)} custom-call(f32[2,128,128]{2,1,0:T(8,128)} %pad_maximum_fusion), custom_call_target="InvertDiagBlocksLowerTriangular" | custom-call | tf_op jit(solution)/shard_map/jit(_cho_solve)/triangular_solve | solution.py:37
  222.7 0.0 all-reduce.11.cloned.1.call-done
  222.7 1.4 fusion.11
  224.1 1.2 convolution_subtract_fusion.1
  225.3 0.3 fusion.23
  225.7 1.0 fusion.22
  226.7 0.4 convolution_subtract_fusion
  227.1 1.2 fusion.19
  228.3 87.9 %all-reduce.7.cloned.1.call-done = bf16[2048,192]{0,1:T(8,128)(2,1)} async-done(((bf16[2048,192]{0,1:T(8,128)(2,1)}), bf16[2048,192]{0,1:T(8,128)(2,1)}) %all-reduce.7.cloned.1.call-update) | async-done | bytes 786448 | tf_op jit(solution)/shard_map/psum | solution.py:30
  316.2 5.1 %mul.27 = f32[2048,4,128]{2,1,0:T(4,128)S(1)} broadcast(f32[2048,4]{1,0:T(8,128)} %copy.12), dimensions={0,1} | broadcast | bytes 4227072 | tf_op jit(solution)/shard_map/mul | solution.py:47
  321.3 3.7 fusion.27
  325.0 2.4 convert_bitcast_fusion
  327.4 56.3 %all_to_all.5 = bf16[32,32,2048]{2,1,0:T(8,128)(2,1)S(1)} all-to-all(bf16[32,32,2048]{2,1,0:T(8,128)(2,1)S(1)} %convert_bitcast_fusion), channel_id=1, replica_groups=mesh['rows'=4,'cols'=32] {'cols'}, dimensions={0} | all-to-all | bytes 8388608 | tf_op jit(solution)/shard_map/all_to_all | solution.py:58
  383.7 1.5 convert_reduce_fusion
  (23 shorter events, 0.2 us)
Async XLA Ops:
  7.2 317.8 %copy-start = (bf16[1024,512]{1,0:T(8,128)(2,1)S(1)}, bf16[1024,512]{1,0:T(8,128)(2,1)}, u32[]{:S(2)}) copy-start(bf16[1024,512]{1,0:T(8,128)(2,1)} %param.11) | copy-start | bytes 3145732
  7.2 10.4 %copy-start.1 = (bf16[2048,512]{1,0:T(8,128)(2,1)S(1)}, bf16[2048,512]{1,0:T(8,128)(2,1)}, u32[]{:S(2)}) copy-start(bf16[2048,512]{1,0:T(8,128)(2,1)} %param.6) | copy-start | bytes 6291460
  7.2 157.3 %all-reduce.9.cloned.1.call-start = ((), (), s32[]{:S(2)}) async-start(), calls=%async_computation.2 | async-start | bytes 393216 | tf_op jit(solution)/shard_map/psum | solution.py:25
  15.5 1.4 copy-start.2
  16.8 8.9 %copy-start.6 = (s32[2048]{0:T(1024)S(1)}, s32[2048]{0:T(1024)}, u32[]{:S(2)}) copy-start(s32[2048]{0:T(1024)} %param.10) | copy-start | bytes 24580
  16.8 206.0 %all-reduce.11.cloned.1.call-start = ((), (), s32[]{:S(2)}) async-start(), calls=%async_computation.3 | async-start | bytes 786432 | tf_op jit(solution)/shard_map/psum | solution.py:29
  17.5 298.7 %all-reduce.7.cloned.1.call-start = ((), (), s32[]{:S(2)}) async-start(), calls=%async_computation.1 | async-start | bytes 1572864 | tf_op jit(solution)/shard_map/psum | solution.py:30
  178.3 0.7 copy-start.5
  222.7 2.6 copy-start.4
  316.2 5.1 %copy-start.3 = (bf16[2048,192]{0,1:T(8,128)(2,1)S(1)}, bf16[2048,192]{0,1:T(8,128)(2,1)}, u32[]{:S(2)}) copy-start(bf16[2048,192]{0,1:T(8,128)(2,1)} %all-reduce.7.cloned.1.call-done) | copy-start | bytes 2359300
Sparse Core Ops, SparseCore 0:
  16.9 147.6 all-reduce.8
  166.9 38.7 all-reduce.10
  209.0 107.2 all-reduce.6
where the time goes:
time: 393 us; the launch traced here: 392 us
  waiting for transfers between devices  225 us (57%)
  other arithmetic  61.9 us (16%)
  blocking collectives  56.3 us (14%)
  matrix products  16.5 us (4%)
  local copies, waits for them, and re-layouts  16.4 us (4%)
  between operations  15.2 us (4%)
    psum x1, waiting for transfers between devices, local(): lax.psum(jnp.dot(own_rows, onehot.astype(jnp.float32), precision=lax.Prec...  137 us
    psum x1, waiting for transfers between devices, local(): lax.psum(jnp.dot(weight, onehot.astype(jnp.bfloat16), preferred_element_t...  87.9 us
    all_to_all x1, blocking collectives, local(): lax.all_to_all(partial, 'cols', split_axis=0, concat_axis=0, tiled=True)  56.3 us
    another operation x7, other arithmetic, local(): factor = jnp.linalg.cholesky(square)  30.1 us
    another operation x6, other arithmetic, local(): coeffs = jax.scipy.linalg.cho_solve((factor, True), panel)  22.7 us
  transfers between devices with their start and end apart: 3, of which 2 were waited for; matrix products, arithmetic and copies ran while one was open for 19% of the time, Pallas kernels for 0%

commit v1 on v0

--- a/solution.py
+++ b/solution.py
@@ -23,8 +23,10 @@
         == (chosen - col_offset)[None, :]
     )
     square = lax.psum(
-        jnp.dot(own_rows, onehot.astype(jnp.float32), precision=lax.Precision.HIGHEST),
-        ("rows", "cols"),
+        lax.psum(
+            jnp.dot(own_rows, onehot.astype(jnp.float32), precision=lax.Precision.HIGHEST), "rows"
+        ),
+        "cols",
     )
     panel = lax.psum(own_rows, "rows")
     weight_cols = lax.psum(

time: 393 us -> 351 us (0.89)
  waiting for transfers between devices: 225 us -> 184 us
    psum x1, waiting for transfers between devices: 0.02 us -> 44.4 us  [local(): panel = lax.psum(own_rows, 'rows')]
    psum x1, waiting for transfers between devices: 87.9 us -> 43.7 us  [local(): lax.psum(jnp.dot(weight, onehot.astype(jnp.bfloat16), preferred_element_t...]
    psum x1, waiting for transfers between devices: 137 us -> 96.1 us  [local(): lax.psum(lax.psum(jnp.dot(own_rows, onehot.astype(jnp.float32), precision...]
  transfers between devices with their start and end apart: 3 -> 3, of which waited for: 2 -> 3; matrix products, arithmetic and copies ran while one was open for 19% -> 21% of each run, Pallas kernels for 0% -> 0%
where the time goes in v1:
time: 351 us
  waiting for transfers between devices  184 us (52%)
  other arithmetic  61.9 us (18%)
  blocking collectives  56.3 us (16%)
  matrix products  16.5 us (5%)
  local copies, waits for them, and re-layouts  16.4 us (5%)
  between operations  15.2 us (4%)
    psum x1, waiting for transfers between devices, local(): lax.psum(lax.psum(jnp.dot(own_rows, onehot.astype(jnp.float32), precision...  96.1 us
    all_to_all x1, blocking collectives, local(): lax.all_to_all(partial, 'cols', split_axis=0, concat_axis=0, tiled=True)  56.3 us
    psum x1, waiting for transfers between devices, local(): panel = lax.psum(own_rows, 'rows')  44.4 us
    psum x1, waiting for transfers between devices, local(): lax.psum(jnp.dot(weight, onehot.astype(jnp.bfloat16), preferred_element_t...  43.7 us
    another operation x7, other arithmetic, local(): factor = jnp.linalg.cholesky(square)  30.1 us
    another operation x6, other arithmetic, local(): coeffs = jax.scipy.linalg.cho_solve((factor, True), panel)  22.7 us
  transfers between devices with their start and end apart: 3, of which 3 were waited for; matrix products, arithmetic and copies ran while one was open for 21% of the time, Pallas kernels for 0%

profile of v1, /device:TPU:1, one launch (start us, length us, event | category | flops | bytes accessed | tf_op | source)
XLA Modules:
  0.0 350.6 jit_solution(7829292902497390477)
XLA Ops:
  7.2 0.0 all-reduce.12.cloned.1.call-start
  7.2 0.8 compare_and_fusion.1
  8.1 0.7 subtract_clamp_fusion
  8.8 0.1 min.18
  8.9 0.1 min.16
  9.0 0.1 and.20
  9.1 0.1 sub.41
  9.2 5.2 %gather_fusion = f32[192,512]{1,0:T(8,128)} fusion(f32[4096,512]{1,0:T(8,128)} %param.7, s32[1024]{0:T(1024)S(1)} %pad_clamp_fusion), kind=kCustom, calls=%fused_computation | custom fusion | bytes 787200 | tf_op jit(solution)/shard_map/jit(_take)/gather | solution.py:19
  14.3 1.1 select_select_fusion
  15.5 1.3 fusion.5
  16.7 0.0 all-reduce.12.cloned.1.call-update
  16.8 0.0 all-reduce.10.cloned.1.call-start
  16.8 44.4 %all-reduce.12.cloned.1.call-done = (f32[192,512]{1,0:T(8,128)}, f32[192,192]{0,1:T(8,128)}) async-done(((f32[192,512]{1,0:T(8,128)}, f32[192,192]{0,1:T(8,128)}), (f32[192,512]{1,0:T(8,128)}, f32[192,192]{0,1:T(8,128)})) %all-reduce.12.cloned.1.call-update) | async-done | bytes 540688 | tf_op jit(solution)/shard_map/psum | solution.py:31
  61.2 0.0 all-reduce.10.cloned.1.call-update
  61.2 0.0 all-reduce.8.cloned.1.call-start
  61.3 1.8 fusion.2
  63.0 0.0 all-reduce.8.cloned.1.call-update
  63.1 0.6 pad_convert_fusion
  63.7 2.5 copy.10
  66.2 3.1 reduce_window_sum.11
  69.3 0.9 fusion.20
  70.2 1.3 copy.12
  71.6 96.1 %all-reduce.10.cloned.1.call-done = f32[192,192]{0,1:T(8,128)} async-done(((f32[192,192]{0,1:T(8,128)}), f32[192,192]{0,1:T(8,128)}) %all-reduce.10.cloned.1.call-update) | async-done | bytes 147472 | tf_op jit(solution)/shard_map/psum | solution.py:25
  167.6 1.0 copy.9
  168.7 1.0 fusion.15
  169.6 11.7 %cholesky.51 = f32[128,128]{1,0:T(8,128)S(1)} custom-call(f32[128,128]{1,0:T(8,128)S(1)} %cholesky.124), custom_call_target="Cholesky" | custom-call | tf_op jit(solution)/shard_map/jit(cholesky)/cholesky | solution.py:38
  181.4 0.6 compare_reduce_fusion.1
  182.1 10.4 %custom-call.18 = f32[1,128,128]{1,2,0:T(8,128)} custom-call(f32[1,128,128]{2,1,0:T(8,128)S(1)} %get-tuple-element.25), custom_call_target="InvertDiagBlocksLowerTriangular" | custom-call | tf_op jit(solution)/shard_map/jit(cholesky)/cholesky | solution.py:38
  192.5 0.9 cholesky.119
  193.3 1.0 constant_dynamic-update-slice_fusion
  194.4 0.8 convolution_subtract_fusion.2
  195.2 6.6 %cholesky.110 = f32[64,64]{1,0:T(8,128)S(1)} custom-call(f32[64,64]{1,0:T(8,128)} %convolution_subtract_fusion.2), custom_call_target="Cholesky" | custom-call | tf_op jit(solution)/shard_map/jit(cholesky)/cholesky | solution.py:38
  201.8 0.6 compare_reduce_fusion
  203.7 0.9 fusion.16
  204.7 0.7 pad_maximum_fusion
  205.3 20.5 %custom-call.19 = f32[2,128,128]{1,2,0:T(8,128)S(1)} custom-call(f32[2,128,128]{2,1,0:T(8,128)} %pad_maximum_fusion), custom_call_target="InvertDiagBlocksLowerTriangular" | custom-call | tf_op jit(solution)/shard_map/jit(_cho_solve)/triangular_solve | solution.py:39
  225.8 1.4 fusion.11
  227.2 1.2 convolution_subtract_fusion.1
  228.4 0.3 fusion.23
  228.8 1.0 fusion.22
  229.8 0.4 convolution_subtract_fusion
  230.2 1.2 fusion.19
  231.4 43.7 %all-reduce.8.cloned.1.call-done = bf16[2048,192]{0,1:T(8,128)(2,1)} async-done(((bf16[2048,192]{0,1:T(8,128)(2,1)}), bf16[2048,192]{0,1:T(8,128)(2,1)}) %all-reduce.8.cloned.1.call-update) | async-done | bytes 786448 | tf_op jit(solution)/shard_map/psum | solution.py:32
  275.1 5.1 %mul.27 = f32[2048,4,128]{2,1,0:T(4,128)S(1)} broadcast(f32[2048,4]{1,0:T(8,128)} %copy.12), dimensions={0,1} | broadcast | bytes 4227072 | tf_op jit(solution)/shard_map/mul | solution.py:49
  280.2 3.7 %fusion.27 = (bf16[2048,512]{1,0:T(8,128)(2,1)}, f32[2048,512]{1,0:T(8,128)S(1)}) fusion(f32[256,8,4,128]{3,2,1,0:T(4,128)S(1)} %bitcast.48, bf16[2048,192]{0,1:T(8,128)(2,1)S(1)} %copy-done.3, f32[64,512]{1,0:T(8,128)S(1)} %fusion.22, f32[128,512]{1,0:T(8,128)S(1)} %fusion.19, bf16[2048,512]{1,0:T(8,128)(2,1)S(1)} %copy-done.1), kind=kOutput, calls=%fused_computation.66 | convolution fusion | flops 2420211712 | bytes 13762560 | tf_op jit(solution)/shard_map/dot_general | solution.py:41
  283.9 2.4 convert_bitcast_fusion
  286.3 56.3 %all_to_all.5 = bf16[32,32,2048]{2,1,0:T(8,128)(2,1)S(1)} all-to-all(bf16[32,32,2048]{2,1,0:T(8,128)(2,1)S(1)} %convert_bitcast_fusion), channel_id=1, replica_groups=mesh['rows'=4,'cols'=32] {'cols'}, dimensions={0} | all-to-all | bytes 8388608 | tf_op jit(solution)/shard_map/all_to_all | solution.py:60
  342.6 1.5 convert_reduce_fusion
  (23 shorter events, 0.2 us)
Async XLA Ops:
  7.2 276.7 %copy-start = (bf16[1024,512]{1,0:T(8,128)(2,1)S(1)}, bf16[1024,512]{1,0:T(8,128)(2,1)}, u32[]{:S(2)}) copy-start(bf16[1024,512]{1,0:T(8,128)(2,1)} %param.11) | copy-start | bytes 3145732
  7.2 54.1 %copy-start.1 = (bf16[2048,512]{1,0:T(8,128)(2,1)S(1)}, bf16[2048,512]{1,0:T(8,128)(2,1)}, u32[]{:S(2)}) copy-start(bf16[2048,512]{1,0:T(8,128)(2,1)} %param.6) | copy-start | bytes 6291460
  7.2 54.0 %all-reduce.12.cloned.1.call-start = ((), (), s32[]{:S(2)}) async-start(), calls=%async_computation.3 | async-start | bytes 1179648 | tf_op jit(solution)/shard_map/psum | solution.py:31
  15.5 1.3 copy-start.2
  16.8 52.6 %copy-start.6 = (s32[2048]{0:T(1024)S(1)}, s32[2048]{0:T(1024)}, u32[]{:S(2)}) copy-start(s32[2048]{0:T(1024)} %param.10) | copy-start | bytes 24580
  16.8 150.9 %all-reduce.10.cloned.1.call-start = ((), (), s32[]{:S(2)}) async-start(), calls=%async_computation.2 | async-start | bytes 393216 | tf_op jit(solution)/shard_map/psum | solution.py:25
  61.2 213.9 %all-reduce.8.cloned.1.call-start = ((), (), s32[]{:S(2)}) async-start(), calls=%async_computation.1 | async-start | bytes 1572864 | tf_op jit(solution)/shard_map/psum | solution.py:32
  181.4 0.7 copy-start.5
  225.8 2.6 copy-start.4
  275.1 5.1 %copy-start.3 = (bf16[2048,192]{0,1:T(8,128)(2,1)S(1)}, bf16[2048,192]{0,1:T(8,128)(2,1)}, u32[]{:S(2)}) copy-start(bf16[2048,192]{0,1:T(8,128)(2,1)} %all-reduce.8.cloned.1.call-done) | copy-start | bytes 2359300
Sparse Core Ops, SparseCore 0:
  16.9 44.2 all-reduce.11
  64.5 103.1 all-reduce.9
  170.9 104.1 all-reduce.7
